TPU v7x, 32 devices: a whole 2x2x4 slice. The times are simulated.
32 devices in a mesh: dp: 2 (over x), expert: 16 (over z, y, core).
Axes of the slice: x: 2, y: 2, z: 4, core: 2. Of those that a mesh axis runs over, the one named last changes fastest.
Arguments:
- tokens: bfloat16 [256, 3584], P(('dp', 'expert')), may hold values from -6 to 6
- cotangent: bfloat16 [256, 3584], P(('dp', 'expert')), may hold values from -6 to 6
- routes: int32 [256, 8], P(('dp', 'expert')), may hold values from 0 to 15, all different within a row; in each aligned block of 8 rows (0 to 7, 8 to 15, ...) at most 6 rows name the same one
- gates: bfloat16 [256, 8], P(('dp', 'expert')), may hold values from 0.049804688 to 1
- w_gate: bfloat16 [16, 3584, 2048], P('expert', None, 'dp'), may hold values from -0.09375 to 0.09375
- w_up: bfloat16 [16, 3584, 2048], P('expert', None, 'dp'), may hold values from -0.09375 to 0.09375
- w_down: bfloat16 [16, 2048, 3584], P('expert', 'dp'), may hold values from -0.125 to 0.125
Outputs:
- grad_tokens: bfloat16 [256, 3584], P(('dp', 'expert'))
- grad_gate: bfloat16 [16, 3584, 2048], P('expert', None, 'dp')
- grad_up: bfloat16 [16, 3584, 2048], P('expert', None, 'dp')
- grad_down: bfloat16 [16, 2048, 3584], P('expert', 'dp')
Inputs may be any that keep to these rules, and one draw needn't show every extreme that they name: `routes`: each row names 8 different experts; among the rows of one device no expert is named more than 6 times, a bound that some block reaches.
All inputs are finite; a program needn't handle non-finite values.
Results may differ from a plain program's by a relative error of at most 0.01.
Values may be sent and summed in bfloat16 or wider, within the bound.
A program may use at most 128 MiB of HBM per device.

v0:
```python
import jax
import jax.numpy as jnp
from jax import lax
from jax.sharding import PartitionSpec as P


def slot_index(flat_ids, expert_count):
    onehot = (flat_ids[..., None] == jnp.arange(expert_count, dtype=jnp.int32)).astype(jnp.int32)
    return jnp.sum((jnp.cumsum(onehot, axis=-2) - onehot) * onehot, axis=-1)


def expert_terms(rows_x, rows_dy, gate_rows, gate_mat, up_mat, down_mat):
    gate_pre = jnp.dot(rows_x, gate_mat, preferred_element_type=jnp.float32)
    up_pre = jnp.dot(rows_x, up_mat, preferred_element_type=jnp.float32)
    sigmoid_g = jax.nn.sigmoid(gate_pre)
    activated = gate_pre * sigmoid_g
    gate_scale = gate_rows.astype(jnp.float32)[:, None]
    hidden = (gate_scale * activated * up_pre).astype(jnp.bfloat16)
    returned = gate_scale * jnp.dot(rows_dy, down_mat.T, preferred_element_type=jnp.float32)
    d_gate = (returned * up_pre * sigmoid_g * (1.0 + gate_pre * (1.0 - sigmoid_g))).astype(
        jnp.bfloat16
    )
    d_up = (returned * activated).astype(jnp.bfloat16)
    grad_gate = jnp.dot(rows_x.T, d_gate, preferred_element_type=jnp.float32)
    grad_up = jnp.dot(rows_x.T, d_up, preferred_element_type=jnp.float32)
    grad_down = jnp.dot(hidden.T, rows_dy, preferred_element_type=jnp.float32)
    return (d_gate, d_up, grad_gate, grad_up, grad_down)


def per_device(tokens, cotangent, routes, gates, w_gate, w_up, w_down):
    tok_rows, features = tokens.shape
    top_k = routes.shape[1]
    expert_count = lax.axis_size("expert")
    capacity = min(tok_rows, (3 * tok_rows * top_k + 2 * expert_count - 1) // (2 * expert_count))
    gate_mat = w_gate[0]
    up_mat = w_up[0]
    down_mat = w_down[0]
    flat_ids = routes.reshape(-1)
    position = flat_ids * capacity + slot_index(flat_ids, expert_count)
    token_of = jnp.arange(tok_rows * top_k, dtype=jnp.int32) // top_k
    slots_all = expert_count * capacity
    send_x = jnp.zeros((slots_all, features), jnp.bfloat16).at[position].set(tokens[token_of])
    send_dy = jnp.zeros((slots_all, features), jnp.bfloat16).at[position].set(cotangent[token_of])
    send_gate = jnp.zeros((slots_all,), jnp.bfloat16).at[position].set(gates.reshape(-1))
    received = (
        lax.all_to_all(
            send_x.reshape(expert_count, capacity, features),
            "expert",
            split_axis=0,
            concat_axis=0,
            tiled=True,
        ),
        lax.all_to_all(
            send_dy.reshape(expert_count, capacity, features),
            "expert",
            split_axis=0,
            concat_axis=0,
            tiled=True,
        ),
        lax.all_to_all(
            send_gate.reshape(expert_count, capacity),
            "expert",
            split_axis=0,
            concat_axis=0,
            tiled=True,
        ),
    )
    gathered = (
        lax.all_gather(received[0], "dp", axis=0, tiled=True),
        lax.all_gather(received[1], "dp", axis=0, tiled=True),
        lax.all_gather(received[2], "dp", axis=0, tiled=True),
    )
    rows_x = gathered[0].reshape(-1, features)
    rows_dy = gathered[1].reshape(-1, features)
    d_gate, d_up, grad_gate, grad_up, grad_down = expert_terms(
        rows_x, rows_dy, gathered[2].reshape(-1), gate_mat, up_mat, down_mat
    )
    own_rows = lax.psum_scatter(
        jnp.dot(d_gate, gate_mat.T, preferred_element_type=jnp.float32)
        + jnp.dot(d_up, up_mat.T, preferred_element_type=jnp.float32),
        "dp",
        scatter_dimension=0,
        tiled=True,
    )
    returned = lax.all_to_all(
        own_rows.reshape(expert_count, capacity, features),
        "expert",
        split_axis=0,
        concat_axis=0,
        tiled=True,
    )
    selected = returned.reshape(slots_all, features)[position]
    grad_x = selected.reshape(tok_rows, top_k, features).sum(axis=1)
    return (
        grad_x.astype(jnp.bfloat16),
        grad_gate.astype(jnp.bfloat16)[None],
        grad_up.astype(jnp.bfloat16)[None],
        grad_down.astype(jnp.bfloat16)[None],
    )


def solution(mesh):
    return jax.shard_map(
        per_device,
        mesh=mesh,
        in_specs=(
            P(("dp", "expert"), None),
            P(("dp", "expert"), None),
            P(("dp", "expert"), None),
            P(("dp", "expert"), None),
            P("expert", None, "dp"),
            P("expert", None, "dp"),
            P("expert", "dp", None),
        ),
        out_specs=(
            P(("dp", "expert"), None),
            P("expert", None, "dp"),
            P("expert", None, "dp"),
            P("expert", "dp", None),
        ),
        check_vma=False,
    )
```

profile of v0, /device:TPU:13, one launch (start us, length us, event | category | flops | bytes accessed | tf_op | source)
XLA Modules:
  0.0 222.9 jit_solution(18376308947812140410)
XLA Ops:
  9.2 2.8 %scatter_custom_fusion.2 = bf16[96,3584]{1,0:T(8,128)(2,1)S(1)} fusion(s32[64]{0:T(128)S(1)} %fusion.30, bf16[8,3584]{1,0:T(8,128)(2,1)S(1)} %copy-done, s32[1024]{0:T(1024)S(1)} %pad_clamp_fusion.1, bf16[]{:T(256)} %constant.26.clone.1), kind=kCustom, calls=%fused_computation.30 | custom fusion | bytes 688130 | tf_op jit(solution)/shard_map/scatter | solution.py:42
  12.2 28.3 %all_to_all.28 = bf16[16,6,3584]{2,1,0:T(8,128)(2,1)S(1)} all-to-all(bf16[16,6,3584]{2,1,0:T(8,128)(2,1)S(1)} %reshape.120), channel_id=1, replica_groups=mesh['dp'=2,'expert'=16] {'expert'}, dimensions={0} | all-to-all | bytes 1376256 | tf_op jit(solution)/shard_map/all_to_all | solution.py:46
  41.6 4.0 %scatter_custom_fusion.1 = bf16[96,3584]{1,0:T(8,128)(2,1)S(1)} fusion(s32[64]{0:T(128)S(1)} %fusion.30, bf16[8,3584]{1,0:T(8,128)(2,1)} %param.8, s32[1024]{0:T(1024)S(1)} %pad_clamp_fusion.1, bf16[]{:T(256)} %constant.26.clone.1), kind=kCustom, calls=%fused_computation.32 | custom fusion | bytes 688640 | tf_op jit(solution)/shard_map/scatter | solution.py:43
  45.9 26.7 %all_to_all.29 = bf16[16,6,3584]{2,1,0:T(8,128)(2,1)S(1)} all-to-all(bf16[16,6,3584]{2,1,0:T(8,128)(2,1)S(1)} %reshape.118), channel_id=1, replica_groups=mesh['dp'=2,'expert'=16] {'expert'}, dimensions={0} | all-to-all | bytes 1376256 | tf_op jit(solution)/shard_map/all_to_all | solution.py:53
  74.9 8.6 %all_to_all.30 = bf16[16,1,6]{2,1,0:T(2,128)(2,1)S(1)} all-to-all(bf16[16,1,6]{2,1,0:T(2,128)(2,1)S(1)} %all_to_all.23), channel_id=1, replica_groups=mesh['dp'=2,'expert'=16] {'expert'}, dimensions={0} | all-to-all | bytes 384 | tf_op jit(solution)/shard_map/all_to_all | solution.py:60
  83.4 4.0 %all-gather = bf16[32,1,6]{2,1,0:T(2,128)(2,1)S(1)} all-gather(bf16[16,1,6]{2,1,0:T(2,128)(2,1)S(1)} %all_to_all.30), channel_id=2, replica_groups=mesh['dp'=2,'expert'=16] {'dp'}, dimensions={0}, use_global_device_ids=true | all-gather | bytes 576 | tf_op jit(solution)/shard_map/all_gather | solution.py:71
  87.7 2.1 copy.20
  89.8 1.3 reshape.121
  91.1 7.2 %all-gather.4.cloned.1.call-done = bf16[32,6,3584]{2,0,1:T(8,128)(2,1)} async-done(((bf16[16,6,3584]{2,0,1:T(8,128)(2,1)}), bf16[32,6,3584]{2,0,1:T(8,128)(2,1)}) %all-gather.4.cloned.1.call-update) | async-done | bytes 1376272 | tf_op jit(solution)/shard_map/all_gather | solution.py:70
  98.3 3.3 %copy.18 = bf16[32,6,3584]{2,1,0:T(8,128)(2,1)} copy(bf16[32,6,3584]{2,0,1:T(8,128)(2,1)} %all-gather.4.cloned.1.call-done) | data formatting | bytes 2752512 | tf_op jit(solution)/shard_map/all_gather | solution.py:70
  101.7 3.7 %reshape.119 = bf16[192,3584]{1,0:T(8,128)(2,1)} reshape(bf16[32,6,3584]{2,1,0:T(8,128)(2,1)} %copy.18) | data formatting | bytes 2752512 | tf_op jit(solution)/shard_map/reshape | solution.py:74
  105.3 5.2 %fusion.2 = f32[192,1024]{1,0:T(8,128)S(1)} fusion(bf16[192,3584]{1,0:T(8,128)(2,1)} %reshape.121, bf16[1,3584,1024]{2,1,0:T(8,128)(2,1)} %param.11), kind=kOutput, calls=%fused_computation.11 | convolution fusion | flops 1409286144 | bytes 9502720 | tf_op jit(solution)/shard_map/dot_general | solution.py:13
  110.7 1.7 fusion.6
  113.1 1.6 slice-done.5
  114.7 2.6 %multiply_convert_fusion.1 = (bf16[192,1024]{1,0:T(8,128)(2,1)S(1)}, bf16[192,1024]{1,0:T(8,128)(2,1)S(1)}) fusion(f32[192,1024]{1,0:T(8,128)S(1)} %fusion.2, f32[192,1024]{1,0:T(8,128)S(1)} %fusion.6, bf16[192,3584]{1,0:T(8,128)(2,1)S(1)} %copy-done.2, bf16[1,1024,3584]{2,1,0:T(8,128)(2,1)S(1)} %bitcast.53, f32[192]{0:T(256)S(1)} %reshape.125), kind=kOutput, calls=%fused_computation.26 | convolution fusion | flops 1412038656 | bytes 11076352 | tf_op jit(solution)/shard_map/dot_general | solution.py:19
  117.4 2.6 %fusion = f32[192,3584]{1,0:T(8,128)S(1)} fusion(bf16[192,1024]{1,0:T(8,128)(2,1)S(1)} %get-tuple-element.5, bf16[1,3584,1024]{2,1,0:T(8,128)(2,1)S(1)} %bitcast.49), kind=kOutput, calls=%fused_computation.9 | convolution fusion | flops 1409286144 | bytes 10485760 | tf_op jit(solution)/shard_map/dot_general | solution.py:79
  120.0 4.2 %fusion.13 = f32[192,3584]{1,0:T(8,128)} fusion(f32[192,3584]{1,0:T(8,128)S(1)} %fusion, bf16[192,1024]{1,0:T(8,128)(2,1)S(1)} %get-tuple-element.4, bf16[1,3584,1024]{2,1,0:T(8,128)(2,1)S(1)} %bitcast.51), kind=kOutput, calls=%fused_computation.22 | convolution fusion | flops 1409974272 | bytes 13238272 | tf_op jit(solution)/shard_map/dot_general | solution.py:80
  124.2 39.3 %reduce-scatter.2.cloned.1.call-done = f32[96,3584]{1,0:T(8,128)} async-done(((f32[192,3584]{1,0:T(8,128)}), f32[96,3584]{1,0:T(8,128)}) %reduce-scatter.2.cloned.1.call-update) | async-done | bytes 1376272 | tf_op jit(solution)/shard_map/reduce_scatter | solution.py:78
  163.4 2.6 %reshape.122 = f32[16,6,3584]{2,1,0:T(8,128)} reshape(f32[96,3584]{1,0:T(8,128)} %reduce-scatter.2.cloned.1.call-done) | data formatting | bytes 2752512 | tf_op jit(solution)/shard_map/reshape | solution.py:86
  166.1 6.5 %all-to-all-start.3 = ((f32[16,6,3584]{2,1,0:T(8,128)}), f32[16,6,3584]{2,1,0:T(8,128)S(1)}, u32[]{:S(2)}, u32[]{:S(2)}) async-start(f32[16,6,3584]{2,1,0:T(8,128)} %reshape.122), calls=%async_computation.4 | async-start | bytes 3670016 | tf_op jit(solution)/shard_map/all_to_all | solution.py:85
  172.6 6.2 %fusion.11 = bf16[1,3584,1024]{2,1,0:T(8,128)(2,1)} fusion(bf16[192,3584]{1,0:T(8,128)(2,1)S(1)} %copy-done.5, bf16[192,1024]{1,0:T(8,128)(2,1)} %copy-done.12), kind=kOutput, calls=%fused_computation.20 | convolution fusion | flops 1412956160 | bytes 9109504 | tf_op jit(solution)/shard_map/dot_general | solution.py:25
  178.8 5.2 %fusion.10 = bf16[1,3584,1024]{2,1,0:T(8,128)(2,1)} fusion(bf16[192,3584]{1,0:T(8,128)(2,1)S(1)} %copy-done.5, bf16[192,1024]{1,0:T(8,128)(2,1)S(1)} %copy-done.11), kind=kOutput, calls=%fused_computation.19 | convolution fusion | flops 1412956160 | bytes 9109504 | tf_op jit(solution)/shard_map/dot_general | solution.py:24
  184.0 5.3 %fusion.12 = bf16[1,1024,3584]{2,1,0:T(8,128)(2,1)} fusion(bf16[192,3584]{1,0:T(8,128)(2,1)S(1)} %copy-done.3, f32[192,1024]{1,0:T(8,128)S(1)} %copy-done.9, f32[192]{0:T(256)S(1)} %reshape.125, f32[192,1024]{1,0:T(8,128)S(1)} %copy-done.7), kind=kOutput, calls=%fused_computation.21 | convolution fusion | flops 1414332416 | bytes 10289920 | tf_op jit(solution)/shard_map/dot_general | solution.py:26
  189.3 25.0 %all-to-all-done.3 = f32[16,6,3584]{2,1,0:T(8,128)S(1)} async-done(((f32[16,6,3584]{2,1,0:T(8,128)}), f32[16,6,3584]{2,1,0:T(8,128)S(1)}, u32[]{:S(2)}, u32[]{:S(2)}) %all-to-all-start.3) | async-done | bytes 1376288 | tf_op jit(solution)/shard_map/all_to_all | solution.py:85
  (71 shorter events, 8.6 us)
Async XLA Ops:
  7.2 2.0 copy-start
  7.2 80.5 %all-gather.6.cloned.1.call-start = ((), (), s32[]{:S(2)}) async-start(), calls=%async_computation.6 | async-start | bytes 2064384 | tf_op jit(solution)/shard_map/all_gather | solution.py:69
  41.6 56.7 %all-gather.4.cloned.1.call-start = ((), (), s32[]{:S(2)}) async-start(), calls=%async_computation.5 | async-start | bytes 2064384 | tf_op jit(solution)/shard_map/all_gather | solution.py:70
  45.6 28.1 %copy-start.13 = (bf16[8,8]{1,0:T(8,128)(2,1)S(1)}, bf16[8,8]{1,0:T(8,128)(2,1)}, u32[]{:S(2)}) copy-start(bf16[8,8]{1,0:T(8,128)(2,1)} %param.10) | copy-start | bytes 388
  73.7 89.8 %reduce-scatter.2.cloned.1.call-start = ((), (), s32[]{:S(2)}) async-start(), calls=%async_computation.7 | async-start | bytes 4128768 | tf_op jit(solution)/shard_map/reduce_scatter | solution.py:78
  101.7 8.9 %slice-start.2 = ((s8[7340032]{0:T(1024)(128)(4,1)}), s8[3145728]{0:T(1024)(128)(4,1)S(1)}, s32[]{:S(2)}) async-start(s8[7340032]{0:T(1024)(128)(4,1)} %bitcast.50), calls=%async_computation.10 | async-start | bytes 6291456
  105.3 5.3 %slice-start.3 = ((s8[7340032]{0:T(1024)(128)(4,1)}), s8[4194304]{0:T(1024)(128)(4,1)S(1)}, s32[]{:S(2)}) async-start(s8[7340032]{0:T(1024)(128)(4,1)} %bitcast.50), calls=%async_computation.11 | async-start | bytes 8388608
  105.3 5.3 %copy-start.4 = (bf16[192,3584]{1,0:T(8,128)(2,1)S(1)}, bf16[192,3584]{1,0:T(8,128)(2,1)}, u32[]{:S(2)}) copy-start(bf16[192,3584]{1,0:T(8,128)(2,1)} %reshape.121) | copy-start | bytes 4128772
  105.3 7.1 %slice-start.4 = ((s8[7340032]{0:T(1024)(128)(4,1)}), s8[4194304]{0:T(1024)(128)(4,1)S(1)}, s32[]{:S(2)}) async-start(s8[7340032]{0:T(1024)(128)(4,1)} %bitcast.52), calls=%async_computation.12 | async-start | bytes 8388608
  105.3 12.0 %slice-start = ((s8[7340032]{0:T(1024)(128)(4,1)}), s8[4194304]{0:T(1024)(128)(4,1)S(1)}, s32[]{:S(2)}) async-start(s8[7340032]{0:T(1024)(128)(4,1)} %bitcast.48), calls=%async_computation.8 | async-start | bytes 8388608
  110.6 1.8 copy-start.6
  110.6 2.4 %copy-start.2 = (bf16[192,3584]{1,0:T(8,128)(2,1)S(1)}, bf16[192,3584]{1,0:T(8,128)(2,1)}, u32[]{:S(2)}) copy-start(bf16[192,3584]{1,0:T(8,128)(2,1)} %reshape.119) | copy-start | bytes 4128772
  110.6 4.1 %slice-start.5 = ((s8[7340032]{0:T(1024)(128)(4,1)}), s8[3145728]{0:T(1024)(128)(4,1)S(1)}, s32[]{:S(2)}) async-start(s8[7340032]{0:T(1024)(128)(4,1)} %bitcast.52), calls=%async_computation.13 | async-start | bytes 6291456
  110.7 6.7 %slice-start.1 = ((s8[7340032]{0:T(1024)(128)(4,1)}), s8[3145728]{0:T(1024)(128)(4,1)S(1)}, s32[]{:S(2)}) async-start(s8[7340032]{0:T(1024)(128)(4,1)} %bitcast.48), calls=%async_computation.9 | async-start | bytes 6291456
  114.7 2.6 %copy-start.8 = (f32[192,1024]{1,0:T(8,128)}, f32[192,1024]{1,0:T(8,128)S(1)}, u32[]{:S(2)}) copy-start(f32[192,1024]{1,0:T(8,128)S(1)} %fusion.6) | copy-start | bytes 2359300
  117.3 2.6 %copy-start.10 = (bf16[192,1024]{1,0:T(8,128)(2,1)}, bf16[192,1024]{1,0:T(8,128)(2,1)S(1)}, u32[]{:S(2)}) copy-start(bf16[192,1024]{1,0:T(8,128)(2,1)S(1)} %get-tuple-element.5) | copy-start | bytes 1179652
  117.3 2.6 %copy-start.12 = (bf16[192,1024]{1,0:T(8,128)(2,1)}, bf16[192,1024]{1,0:T(8,128)(2,1)S(1)}, u32[]{:S(2)}) copy-start(bf16[192,1024]{1,0:T(8,128)(2,1)S(1)} %get-tuple-element.4) | copy-start | bytes 1179652
  124.2 48.4 %copy-start.5 = (bf16[192,3584]{1,0:T(8,128)(2,1)S(1)}, bf16[192,3584]{1,0:T(8,128)(2,1)}, u32[]{:S(2)}) copy-start(bf16[192,3584]{1,0:T(8,128)(2,1)} %reshape.121) | copy-start | bytes 4128772
  166.1 48.3 %all-to-all-start.3 = ((f32[16,6,3584]{2,1,0:T(8,128)}), f32[16,6,3584]{2,1,0:T(8,128)S(1)}, u32[]{:S(2)}, u32[]{:S(2)}) async-start(f32[16,6,3584]{2,1,0:T(8,128)} %reshape.122), calls=%async_computation.4 | async-start | bytes 3670016 | tf_op jit(solution)/shard_map/all_to_all | solution.py:85
  172.6 6.2 %copy-start.11 = (bf16[192,1024]{1,0:T(8,128)(2,1)S(1)}, bf16[192,1024]{1,0:T(8,128)(2,1)}, u32[]{:S(2)}) copy-start(bf16[192,1024]{1,0:T(8,128)(2,1)} %copy-done.10) | copy-start | bytes 1179652
  178.8 5.2 %copy-start.3 = (bf16[192,3584]{1,0:T(8,128)(2,1)S(1)}, bf16[192,3584]{1,0:T(8,128)(2,1)}, u32[]{:S(2)}) copy-start(bf16[192,3584]{1,0:T(8,128)(2,1)} %reshape.119) | copy-start | bytes 4128772
  178.8 5.2 %copy-start.7 = (f32[192,1024]{1,0:T(8,128)S(1)}, f32[192,1024]{1,0:T(8,128)}, u32[]{:S(2)}) copy-start(f32[192,1024]{1,0:T(8,128)} %copy-done.6) | copy-start | bytes 2359300
  178.8 5.2 %copy-start.9 = (f32[192,1024]{1,0:T(8,128)S(1)}, f32[192,1024]{1,0:T(8,128)}, u32[]{:S(2)}) copy-start(f32[192,1024]{1,0:T(8,128)} %copy-done.8) | copy-start | bytes 2359300
  214.4 2.0 copy-start.1
Sparse Core Ops, SparseCore 0:
  41.7 24.3 all-gather.5
  73.8 24.5 all-gather.3
  124.3 39.1 reduce-scatter.1
where the time goes:
time: 223 us
  waiting for transfers between devices  71.6 us (32%)
  blocking collectives  67.6 us (30%)
  matrix products  33 us (15%)
  local copies, waits for them, and re-layouts  28 us (13%)
  between operations  14.1 us (6%)
  starting transfers between devices  6.63 us (3%)
    reduce_scatter x1, waiting for transfers between devices, per_device(): lax.psum_scatter(jnp.dot(d_gate, gate_mat.T, preferred_element_type=jnp.f...  39.3 us
    all_to_all x1, blocking collectives, per_device(): lax.all_to_all(send_x.reshape(expert_count, capacity, features), 'expert'...  28.3 us
    all_to_all x1, blocking collectives, per_device(): lax.all_to_all(send_dy.reshape(expert_count, capacity, features), 'expert...  26.7 us
    all_to_all x1, waiting for transfers between devices, per_device(): lax.all_to_all(own_rows.reshape(expert_count, capacity, features), 'exper...  25 us
    all_to_all x1, blocking collectives, per_device(): lax.all_to_all(send_gate.reshape(expert_count, capacity), 'expert', split...  8.57 us
    all_gather x1, waiting for transfers between devices, per_device(): lax.all_gather(received[1], 'dp', axis=0, tiled=True)  7.24 us
    scatter x2, local copies, waits for them, and re-layouts, per_device(): jnp.zeros((slots_all, features), jnp.bfloat16).at[position]  6.78 us
    all_to_all x1, starting transfers between devices, per_device(): lax.all_to_all(own_rows.reshape(expert_count, capacity, features), 'exper...  6.5 us
  transfers between devices with their start and end apart: 4, of which 3 were waited for; matrix products, arithmetic and copies ran while one was open for 12% of the time, Pallas kernels for 0%

commit v1 on v0

--- a/solution.py
+++ b/solution.py
@@ -1,6 +1,10 @@
+import functools
+
 import jax
 import jax.numpy as jnp
 from jax import lax
+from jax.experimental import pallas as pl
+from jax.experimental.pallas import tpu as pltpu
 from jax.sharding import PartitionSpec as P
 
 
@@ -27,7 +31,7 @@
     return (d_gate, d_up, grad_gate, grad_up, grad_down)
 
 
-def per_device(tokens, cotangent, routes, gates, w_gate, w_up, w_down):
+def routed_per_device(tokens, cotangent, routes, gates, w_gate, w_up, w_down):
     tok_rows, features = tokens.shape
     top_k = routes.shape[1]
     expert_count = lax.axis_size("expert")
@@ -99,6 +103,111 @@
     )
 
 
+LANES = 128
+NT = (((1,), (1,)), ((), ()))
+
+
+def pick(options, size):
+    return next((o for o in options if size % o == 0), size)
+
+
+def main_kernel(tile, sel_ref, x_ref, dy_ref, coef_ref, wg_ref, wu_ref, wd_ref, p_ref, gg_ref, gu_ref, gd_ref, xt_ref, acc_ref):
+    step = pl.program_id(0)
+    features = x_ref.shape[1]
+
+    @pl.when(step == 0)
+    def _():
+        for t in range(0, features, tile):
+            xt_ref[t:t + tile, :] = x_ref[:, t:t + tile].T
+
+    c = jnp.sum(coef_ref[...].astype(jnp.float32) * sel_ref[...], axis=1, keepdims=True)
+    x = x_ref[...]
+    g = jnp.dot(x, wg_ref[...], preferred_element_type=jnp.float32)
+    u = jnp.dot(x, wu_ref[...], preferred_element_type=jnp.float32)
+    r = c * lax.dot_general(dy_ref[...], wd_ref[...], NT, preferred_element_type=jnp.float32)
+    s = jax.nn.sigmoid(g)
+    act = g * s
+    hid_t = (c * act * u).astype(jnp.bfloat16).T
+    dg = (r * u * s * (1.0 + g * (1.0 - s))).astype(jnp.bfloat16)
+    du = (r * act).astype(jnp.bfloat16)
+
+    for t in range(0, features, tile):
+        cols = slice(t, t + tile)
+        part = lax.dot_general(dg, wg_ref[cols, :], NT, preferred_element_type=jnp.float32)
+        part += lax.dot_general(du, wu_ref[cols, :], NT, preferred_element_type=jnp.float32)
+
+        @pl.when(step == 0)
+        def _():
+            acc_ref[:, cols] = part
+
+        @pl.when(step > 0)
+        def _():
+            acc_ref[:, cols] += part
+
+        gg_ref[cols, :] = jnp.dot(xt_ref[cols, :], dg, preferred_element_type=jnp.float32).astype(jnp.bfloat16)
+        gu_ref[cols, :] = jnp.dot(xt_ref[cols, :], du, preferred_element_type=jnp.float32).astype(jnp.bfloat16)
+        gd_ref[:, cols] = jnp.dot(hid_t, dy_ref[:, cols], preferred_element_type=jnp.float32).astype(jnp.bfloat16)
+
+    @pl.when(step == pl.num_programs(0) - 1)
+    def _():
+        p_ref[...] = acc_ref[...].astype(jnp.bfloat16)
+
+
+def main_call(sel, gathered, w_gate, w_up, w_down):
+    _, features, hidden = w_gate.shape
+    rows = gathered.shape[0]
+    chunk = pick((256, 128), hidden)
+    tile = pick((512, 256, 128), features)
+    whole = lambda width, index: pl.BlockSpec((rows, width), lambda i: (0, index), pipeline_mode=pl.Buffered(1))
+    col = pl.BlockSpec((None, features, chunk), lambda i: (0, 0, i))
+    row = pl.BlockSpec((None, chunk, features), lambda i: (0, i, 0))
+    bf = jnp.bfloat16
+    return pl.pallas_call(
+        functools.partial(main_kernel, tile),
+        grid=(hidden // chunk,),
+        in_specs=[
+            pl.BlockSpec((1, LANES), lambda i: (0, 0)),
+            whole(features, 0), whole(features, 1), whole(LANES, 2 * features // LANES),
+            col, col, row,
+        ],
+        out_specs=[pl.BlockSpec((rows, features), lambda i: (0, 0)), col, col, row],
+        out_shape=[
+            jax.ShapeDtypeStruct((rows, features), bf),
+            jax.ShapeDtypeStruct(w_gate.shape, bf),
+            jax.ShapeDtypeStruct(w_up.shape, bf),
+            jax.ShapeDtypeStruct(w_down.shape, bf),
+        ],
+        scratch_shapes=[pltpu.VMEM((features, rows), bf), pltpu.VMEM((rows, features), jnp.float32)],
+        compiler_params=pltpu.CompilerParams(dimension_semantics=("arbitrary",), vmem_limit_bytes=60 << 20),
+    )(sel, gathered, gathered, gathered, w_gate, w_up, w_down)
+
+
+def payload_of(tokens, cotangent, routes, gates):
+    lanes = jnp.arange(LANES, dtype=jnp.int32)
+    hit = routes[:, :, None] == lanes[None, None, :]
+    coef = jnp.sum(jnp.where(hit, gates[:, :, None].astype(jnp.float32), 0.0), axis=1)
+    return jnp.concatenate([tokens, cotangent, coef.astype(jnp.bfloat16)], axis=1)
+
+
+def dense_per_device(tokens, cotangent, routes, gates, w_gate, w_up, w_down):
+    payload = payload_of(tokens, cotangent, routes, gates)
+    gathered = lax.all_gather(payload, ("dp", "expert"), axis=0, tiled=True)
+    sel = (jnp.arange(LANES, dtype=jnp.int32) == lax.axis_index("expert")).astype(jnp.float32)[None]
+    partial, grad_gate, grad_up, grad_down = main_call(sel, gathered, w_gate, w_up, w_down)
+    grad_x = lax.psum_scatter(partial, ("dp", "expert"), scatter_dimension=0, tiled=True)
+    return grad_x, grad_gate, grad_up, grad_down
+
+
+def per_device(tokens, cotangent, routes, gates, w_gate, w_up, w_down):
+    features = tokens.shape[1]
+    rows = tokens.shape[0] * lax.axis_size("dp") * lax.axis_size("expert")
+    chunk = pick((256, 128), w_gate.shape[2])
+    need = features * (14 * rows + 24 * chunk)
+    fits = need < (56 << 20) and lax.axis_size("expert") <= LANES and features % LANES == 0
+    body = dense_per_device if fits else routed_per_device
+    return body(tokens, cotangent, routes, gates, w_gate, w_up, w_down)
+
+
 def solution(mesh):
     return jax.shard_map(
         per_device,

time: 223 us -> 253 us (1.13)
  the two profiles are of different devices: /device:TPU:13 before, /device:TPU:0 now
where the time goes in v1:
time: 253 us; the launch traced here: 252 us
  waiting for transfers between devices  201 us (79%)
  Pallas kernels  33.8 us (13%)
  between operations  14 us (6%)
  other arithmetic  3.48 us (1%)
    reduce_scatter x1, waiting for transfers between devices, dense_per_device(): lax.psum_scatter(partial, ('dp', 'expert'), scatter_dimension=0, tiled=True)  137 us
    all_gather x1, waiting for transfers between devices, dense_per_device(): gathered = lax.all_gather(payload, ('dp', 'expert'), axis=0, tiled=True)  64 us
    pallas_call x1, Pallas kernels, main_call(): pl.pallas_call(functools.partial(main_kernel, tile), grid=(hidden // chun...  33.8 us
  transfers between devices with their start and end apart: 2, of which 2 were waited for; matrix products, arithmetic and copies ran while one was open for 0% of the time, Pallas kernels for 0%

profile of v1, /device:TPU:0, one launch (start us, length us, event | category | flops | bytes accessed | tf_op | source)
XLA Modules:
  0.0 252.5 jit_solution(1527103816012677087)
XLA Ops:
  7.2 0.0 all-gather.2.cloned.1.call-start
  7.2 0.7 convert_element_type.18
  7.9 0.8 select_reduce_fusion
  8.7 1.5 pad_maximum_fusion
  10.2 0.0 all-gather.2.cloned.1.call-update
  10.2 0.0 reduce-scatter.2.cloned.1.call-start
  10.3 0.5 compare_convert_fusion.sel_ref
  10.8 64.0 %all-gather.2.cloned.1.call-done.x_ref.dy_ref.coef_ref = bf16[256,7296]{1,0:T(8,128)(2,1)} async-done(((bf16[8,7296]{1,0:T(8,128)(2,1)}), bf16[256,7296]{1,0:T(8,128)(2,1)}) %all-gather.2.cloned.1.call-update) | async-done | bytes 3735568 | tf_op jit(solution)/shard_map/all_gather | solution.py:194
  74.8 33.8 %shard_map.102 = (bf16[256,3584]{1,0:T(8,128)(2,1)}, bf16[1,3584,1024]{2,1,0:T(8,128)(2,1)}, bf16[1,3584,1024]{2,1,0:T(8,128)(2,1)}, bf16[1,1024,3584]{2,1,0:T(8,128)(2,1)}) custom-call(f32[1,128]{1,0:T(1,128)} %compare_convert_fusion.sel_ref, bf16[256,7296]{1,0:T(8,128)(2,1)} %all-gather.2.cloned.1.call-done.x_ref.dy_ref.coef_ref, ...), custom_call_target="tpu_custom_call" | custom-call | tf_op jit(solution)/shard_map/pallas_call | solution.py:165
  108.6 0.0 reduce-scatter.2.cloned.1.call-update
  108.6 137.1 %reduce-scatter.2.cloned.1.call-done = bf16[8,3584]{1,0:T(8,128)(2,1)} async-done(((bf16[256,3584]{1,0:T(8,128)(2,1)}), bf16[8,3584]{1,0:T(8,128)(2,1)}) %reduce-scatter.2.cloned.1.call-update) | async-done | bytes 57360 | tf_op jit(solution)/shard_map/reduce_scatter | solution.py:197
Async XLA Ops:
  7.2 67.6 %all-gather.2.cloned.1.call-start = ((), (), s32[]{:S(2)}) async-start(), calls=%async_computation.1 | async-start | bytes 3852288 | tf_op jit(solution)/shard_map/all_gather | solution.py:194
  10.2 235.4 %reduce-scatter.2.cloned.1.call-start = ((), (), s32[]{:S(2)}) async-start(), calls=%async_computation.2 | async-start | bytes 1892352 | tf_op jit(solution)/shard_map/reduce_scatter | solution.py:197
Sparse Core Ops, SparseCore 0:
  11.4 63.3 all-gather.1
  108.7 136.8 reduce-scatter.1

commit v2 on v1

--- a/solution.py
+++ b/solution.py
@@ -1,7 +1,10 @@
 import functools
+import itertools
+import math
 
 import jax
 import jax.numpy as jnp
+import numpy as np
 from jax import lax
 from jax.experimental import pallas as pl
 from jax.experimental.pallas import tpu as pltpu
@@ -155,10 +158,10 @@
 
 def main_call(sel, gathered, w_gate, w_up, w_down):
     _, features, hidden = w_gate.shape
-    rows = gathered.shape[0]
+    rows = gathered[0].shape[0]
     chunk = pick((256, 128), hidden)
     tile = pick((512, 256, 128), features)
-    whole = lambda width, index: pl.BlockSpec((rows, width), lambda i: (0, index), pipeline_mode=pl.Buffered(1))
+    whole = lambda width: pl.BlockSpec((rows, width), lambda i: (0, 0), pipeline_mode=pl.Buffered(1))
     col = pl.BlockSpec((None, features, chunk), lambda i: (0, 0, i))
     row = pl.BlockSpec((None, chunk, features), lambda i: (0, i, 0))
     bf = jnp.bfloat16
@@ -167,7 +170,7 @@
         grid=(hidden // chunk,),
         in_specs=[
             pl.BlockSpec((1, LANES), lambda i: (0, 0)),
-            whole(features, 0), whole(features, 1), whole(LANES, 2 * features // LANES),
+            whole(features), whole(features), whole(LANES),
             col, col, row,
         ],
         out_specs=[pl.BlockSpec((rows, features), lambda i: (0, 0)), col, col, row],
@@ -179,38 +182,311 @@
         ],
         scratch_shapes=[pltpu.VMEM((features, rows), bf), pltpu.VMEM((rows, features), jnp.float32)],
         compiler_params=pltpu.CompilerParams(dimension_semantics=("arbitrary",), vmem_limit_bytes=60 << 20),
-    )(sel, gathered, gathered, gathered, w_gate, w_up, w_down)
-
-
-def payload_of(tokens, cotangent, routes, gates):
+    )(sel, *gathered, w_gate, w_up, w_down)
+
+
+def digits_of(mesh):
+    digits = {}
+    for number, axis in enumerate(mesh.axis_names):
+        line = np.moveaxis(mesh.devices, number, 0)
+        line = line.reshape(line.shape[0], -1)[:, 0]
+        places = [(*d.coords, d.core_on_chip) for d in line]
+        stride = 1
+        while stride < len(places):
+            name = next(i for i in range(4) if places[stride][i] != places[0][i])
+            size = len({p[name] for p in places})
+            digits[name] = (axis, stride, size)
+            stride *= size
+    return digits
+
+
+class Torus:
+    def __init__(self, digits, axis_sizes):
+        self.digits, self.axis_sizes = digits, axis_sizes
+        self.me = {n: (lax.axis_index(a) // s) % k for n, (a, s, k) in digits.items()}
+
+    def at(self, delta):
+        place = dict(self.me)
+        for name, step in delta.items():
+            size = self.digits[name][2]
+            place[name] = (self.me[name] + step) % 2 if size == 2 else self.me[name] + step
+        return place
+
+    def device(self, place):
+        index = {a: 0 for a in self.axis_sizes}
+        for name, (axis, stride, _) in self.digits.items():
+            index[axis] = index[axis] + place[name] * stride
+        return index
+
+    def linear(self, place):
+        index, total = self.device(place), 0
+        for axis, size in self.axis_sizes.items():
+            total = total * size + index[axis]
+        return total
+
+    def steps(self, name):
+        return (1,) if self.digits[name][2] == 2 else (1, -1)
+
+    def inside(self, name, step):
+        size = self.digits[name][2]
+        if size == 2 or step == 0:
+            return None
+        return self.me[name] + step < size if step > 0 else self.me[name] + step >= 0
+
+    def sites(self, order):
+        spans = []
+        for name in order:
+            size = self.digits[name][2]
+            spans.append(range(size) if size == 2 else range(1 - size, size))
+        return [dict(zip(order, combo)) for combo in itertools.product(*spans)]
+
+    def valid(self, delta):
+        found = None
+        for name, step in delta.items():
+            test = self.inside(name, step)
+            if test is not None:
+                found = test if found is None else jnp.logical_and(found, test)
+        return found
+
+    def children(self, order, delta):
+        last = max([i for i, n in enumerate(order) if delta[n]], default=-1)
+        found = []
+        if last >= 0 and self.digits[order[last]][2] > 2:
+            found.append((order[last], -1 if delta[order[last]] > 0 else 1))
+        for name in order[last + 1:]:
+            found += [(name, step) for step in self.steps(name)]
+        return found
+
+    def parent(self, order, delta):
+        last = max(i for i, n in enumerate(order) if delta[n])
+        return order[last], 1 if delta[order[last]] > 0 else -1
+
+    def barrier(self):
+        sem = pltpu.get_barrier_semaphore()
+        count = 0
+        for name in self.digits:
+            for step in self.steps(name):
+                test = self.inside(name, step)
+                target = self.device(self.at({name: step}))
+
+                def greet(target=target):
+                    pl.semaphore_signal(sem, inc=1, device_id=target, device_id_type=pl.DeviceIdType.MESH)
+
+                when(test, greet)
+                count = count + (1 if test is None else test.astype(jnp.int32))
+        pl.semaphore_wait(sem, count)
+
+
+def when(test, body):
+    if test is None:
+        body()
+    else:
+        pl.when(test)(body)
+
+
+def distance(delta):
+    return sum(abs(v) for v in delta.values())
+
+
+def lines_and_pairs(digits):
+    lines = [n for n in digits if digits[n][2] > 2]
+    pairs = [n for n in digits if digits[n][2] == 2 and n != 3]
+    core = [3] if 3 in digits else []
+    return tuple(lines + pairs + core), tuple(lines + pairs[::-1] + core)
+
+
+def gather_kernel(digits, axis_sizes, orders, *refs):
+    parts = len(orders)
+    ins, outs = refs[:parts], refs[parts:2 * parts]
+    send_sem, recv_sem, local_sem = refs[2 * parts:]
+    torus = Torus(digits, axis_sizes)
+    rows = ins[0].shape[0]
+
+    def block(ref, index):
+        return ref.at[pl.ds(pl.multiple_of(index * rows, rows), rows)]
+
+    mine = torus.linear(torus.me)
+    own = [pltpu.make_async_copy(ins[p], block(outs[p], mine), local_sem.at[p]) for p in range(parts)]
+    torus.barrier()
+    plan, used = [], [0] * parts
+    for p in range(parts):
+        for delta in torus.sites(orders[p]):
+            plan.append((distance(delta), p, delta))
+    plan.sort(key=lambda entry: entry[:2])
+    later = []
+    for _, p, delta in plan:
+        index = torus.linear(torus.at(delta))
+        root = distance(delta) == 0
+        copies = []
+        for name, step in torus.children(orders[p], delta):
+            copies.append((torus.inside(name, step), pltpu.make_async_remote_copy(
+                src_ref=ins[p] if root else block(outs[p], index),
+                dst_ref=block(outs[p], index),
+                send_sem=send_sem.at[p, used[p]],
+                recv_sem=recv_sem.at[p, index],
+                device_id=torus.device(torus.at({name: step})),
+                device_id_type=pl.DeviceIdType.MESH,
+            )))
+            used[p] += 1
+
+        def handle(p=p, index=index, root=root, copies=copies):
+            if not root:
+                pltpu.make_async_copy(ins[p], block(outs[p], index), recv_sem.at[p, index]).wait()
+            for test, copy in copies:
+                when(test, copy.start)
+
+        def finish(copies=copies):
+            for test, copy in copies:
+                when(test, copy.wait_send)
+
+        test = torus.valid(delta)
+        when(test, handle)
+        later.append((test, finish))
+        if root:
+            own[p].start()
+    for test, finish in later:
+        when(test, finish)
+    for copy in own:
+        copy.wait()
+
+
+def gather_call(digits, axis_sizes, arrays):
+    first, second = lines_and_pairs(digits)
+    orders = (first, second) + (first,) * (len(arrays) - 2)
+    devices = math.prod(axis_sizes.values())
+    count = max(count_sends(digits, order) for order in orders)
+    return pl.pallas_call(
+        functools.partial(gather_kernel, digits, axis_sizes, orders),
+        in_specs=[pl.BlockSpec(memory_space=pl.ANY)] * len(arrays),
+        out_specs=[pl.BlockSpec(memory_space=pl.ANY)] * len(arrays),
+        out_shape=[jax.ShapeDtypeStruct((devices * a.shape[0], a.shape[1]), a.dtype) for a in arrays],
+        scratch_shapes=[
+            pltpu.SemaphoreType.DMA((len(arrays), count)),
+            pltpu.SemaphoreType.DMA((len(arrays), devices)),
+            pltpu.SemaphoreType.DMA((len(arrays),)),
+        ],
+        compiler_params=pltpu.CompilerParams(collective_id=0, has_side_effects=True),
+    )(*arrays)
+
+
+def count_sends(digits, order):
+    shape = Torus.__new__(Torus)
+    shape.digits = digits
+    return sum(len(shape.children(order, delta)) for delta in shape.sites(order))
+
+
+def scatter_kernel(digits, axis_sizes, orders, ways, p_ref, out_ref, land, total, total32, send_sem, recv_sem):
+    torus = Torus(digits, axis_sizes)
+    parts = len(orders)
+    width = p_ref.shape[2] // parts
+    plan = []
+    for p in range(parts):
+        for number, delta in enumerate(torus.sites(orders[p])):
+            plan.append((len(torus.children(orders[p], delta)), -distance(delta), p, number, delta))
+    plan.sort(key=lambda entry: entry[:4])
+    torus.barrier()
+    later = []
+    for _, _, p, number, delta in plan:
+        order = orders[p]
+        index = torus.linear(torus.at(delta))
+        cols = slice(p * width, (p + 1) * width)
+        root = distance(delta) == 0
+        kids = torus.children(order, delta)
+        source = total if kids else p_ref
+        copy = None
+        if not root:
+            name, step = torus.parent(order, delta)
+            way = ways.index((name, step if digits[name][2] == 2 else -step))
+            copy = pltpu.make_async_remote_copy(
+                src_ref=source.at[index, :, cols],
+                dst_ref=land.at[way, index, :, cols],
+                send_sem=send_sem.at[p, number],
+                recv_sem=recv_sem.at[p, way, index],
+                device_id=torus.device(torus.at({name: step})),
+                device_id_type=pl.DeviceIdType.MESH,
+            )
+
+        def handle(p=p, index=index, cols=cols, kids=kids, copy=copy):
+            if kids:
+                total32[:, cols] = p_ref[index, :, cols].astype(jnp.float32)
+                for name, step in kids:
+                    way = ways.index((name, step))
+
+                    def add(way=way):
+                        here = land.at[way, index, :, cols]
+                        pltpu.make_async_copy(here, here, recv_sem.at[p, way, index]).wait()
+                        total32[:, cols] += land[way, index, :, cols].astype(jnp.float32)
+
+                    when(torus.inside(name, step), add)
+                if copy is None:
+                    out_ref[:, cols] = total32[:, cols].astype(out_ref.dtype)
+                else:
+                    total[index, :, cols] = total32[:, cols].astype(total.dtype)
+            if copy is not None:
+                copy.start()
+
+        test = torus.valid(delta)
+        when(test, handle)
+        if copy is not None:
+            later.append((test, copy.wait_send))
+    for test, finish in later:
+        when(test, finish)
+
+
+def scatter_call(digits, axis_sizes, partial):
+    orders = lines_and_pairs(digits)
+    ways = [(n, s) for n, d in digits.items() for s in ((1,) if d[2] == 2 else (1, -1))]
+    devices = math.prod(axis_sizes.values())
+    rows, features = partial.shape[0] // devices, partial.shape[1]
+    shape = Torus.__new__(Torus)
+    shape.digits = digits
+    count = len(shape.sites(orders[0]))
+    vmem = pl.BlockSpec(memory_space=pltpu.VMEM)
+    return pl.pallas_call(
+        functools.partial(scatter_kernel, digits, axis_sizes, orders, ways),
+        in_specs=[vmem],
+        out_specs=vmem,
+        out_shape=jax.ShapeDtypeStruct((rows, features), partial.dtype),
+        scratch_shapes=[
+            pltpu.VMEM((len(ways), devices, rows, features), partial.dtype),
+            pltpu.VMEM((devices, rows, features), partial.dtype),
+            pltpu.VMEM((rows, features), jnp.float32),
+            pltpu.SemaphoreType.DMA((2, count)),
+            pltpu.SemaphoreType.DMA((2, len(ways), devices)),
+        ],
+        compiler_params=pltpu.CompilerParams(collective_id=1, has_side_effects=True, vmem_limit_bytes=40 << 20),
+    )(partial.reshape(devices, rows, features))
+
+
+def coef_of(routes, gates):
     lanes = jnp.arange(LANES, dtype=jnp.int32)
     hit = routes[:, :, None] == lanes[None, None, :]
     coef = jnp.sum(jnp.where(hit, gates[:, :, None].astype(jnp.float32), 0.0), axis=1)
-    return jnp.concatenate([tokens, cotangent, coef.astype(jnp.bfloat16)], axis=1)
-
-
-def dense_per_device(tokens, cotangent, routes, gates, w_gate, w_up, w_down):
-    payload = payload_of(tokens, cotangent, routes, gates)
-    gathered = lax.all_gather(payload, ("dp", "expert"), axis=0, tiled=True)
+    return coef.astype(jnp.bfloat16)
+
+
+def dense_per_device(digits, axis_sizes, tokens, cotangent, routes, gates, w_gate, w_up, w_down):
+    gathered = gather_call(digits, axis_sizes, (tokens, cotangent, coef_of(routes, gates)))
     sel = (jnp.arange(LANES, dtype=jnp.int32) == lax.axis_index("expert")).astype(jnp.float32)[None]
     partial, grad_gate, grad_up, grad_down = main_call(sel, gathered, w_gate, w_up, w_down)
-    grad_x = lax.psum_scatter(partial, ("dp", "expert"), scatter_dimension=0, tiled=True)
+    grad_x = scatter_call(digits, axis_sizes, partial)
     return grad_x, grad_gate, grad_up, grad_down
 
 
-def per_device(tokens, cotangent, routes, gates, w_gate, w_up, w_down):
+def per_device(digits, axis_sizes, tokens, cotangent, routes, gates, w_gate, w_up, w_down):
     features = tokens.shape[1]
-    rows = tokens.shape[0] * lax.axis_size("dp") * lax.axis_size("expert")
+    rows = tokens.shape[0] * math.prod(axis_sizes.values())
     chunk = pick((256, 128), w_gate.shape[2])
     need = features * (14 * rows + 24 * chunk)
-    fits = need < (56 << 20) and lax.axis_size("expert") <= LANES and features % LANES == 0
-    body = dense_per_device if fits else routed_per_device
-    return body(tokens, cotangent, routes, gates, w_gate, w_up, w_down)
+    fits = need < (56 << 20) and axis_sizes["expert"] <= LANES and features % (2 * LANES) == 0
+    args = (tokens, cotangent, routes, gates, w_gate, w_up, w_down)
+    return dense_per_device(digits, axis_sizes, *args) if fits else routed_per_device(*args)
 
 
 def solution(mesh):
+    body = functools.partial(per_device, digits_of(mesh), dict(mesh.shape))
     return jax.shard_map(
-        per_device,
+        body,
         mesh=mesh,
         in_specs=(
             P(("dp", "expert"), None),

time: 253 us -> 91.9 us (0.36)
  waiting for transfers between devices: 201 us -> 0 us
  Pallas kernels: 33.8 us -> 86.4 us
  between operations: 14 us -> 0.65 us
    reduce_scatter x1 -> x0, waiting for transfers between devices: 137 us -> none  [dense_per_device(): lax.psum_scatter(partial, ('dp', 'expert'), scatter_dimension=0, tiled=True)]
    all_gather x1 -> x0, waiting for transfers between devices: 64 us -> none  [dense_per_device(): gathered = lax.all_gather(payload, ('dp', 'expert'), axis=0, tiled=True)]
    pallas_call x0 -> x2, Pallas kernels: none -> 52.6 us  [the longest x1 30.4 us: gather_call(): pl.pallas_call(functools.partial(gather_kernel, digits, axis_sizes, order...]
  transfers between devices with their start and end apart: 2 -> 0, of which waited for: 2 -> 0; matrix products, arithmetic and copies ran while one was open for 0% -> 0% of each run, Pallas kernels for 0% -> 0%
where the time goes in v2:
time: 91.9 us; the launch traced here: 91.7 us
  Pallas kernels  86.4 us (94%)
  other arithmetic  2.56 us (3%)
  local copies, waits for them, and re-layouts  2.12 us (2%)
    pallas_call x1, Pallas kernels, main_call(): pl.pallas_call(functools.partial(main_kernel, tile), grid=(hidden // chun...  33.8 us
    pallas_call x1, Pallas kernels, gather_call(): pl.pallas_call(functools.partial(gather_kernel, digits, axis_sizes, order...  30.4 us
    pallas_call x1, Pallas kernels, scatter_call(): pl.pallas_call(functools.partial(scatter_kernel, digits, axis_sizes, orde...  22.2 us
    unnamed x3, local copies, waits for them, and re-layouts  2.12 us

profile of v2, /device:TPU:0, one launch (start us, length us, event | category | flops | bytes accessed | tf_op | source)
XLA Modules:
  0.0 91.7 jit_solution(9349355438443661367)
XLA Ops:
  0.6 0.5 compare_convert_fusion.sel_ref
  1.1 0.7 convert_element_type.18
  1.8 1.4 %select_reduce_fusion.refs_2_ = bf16[8,128]{1,0:T(8,128)(2,1)} fusion(f32[8,8]{1,0:T(8,128)S(1)} %convert_element_type.18, s32[8,8]{1,0:T(8,128)} %param.9), kind=kLoop, calls=%fused_computation | loop fusion | flops 23552 | bytes 2560 | tf_op jit(solution)/shard_map/reduce_sum | solution.py:464
  3.2 30.4 %shard_map.102 = (bf16[256,3584]{1,0:T(8,128)(2,1)}, bf16[256,3584]{1,0:T(8,128)(2,1)}, bf16[256,128]{1,0:T(8,128)(2,1)}) custom-call(bf16[8,3584]{1,0:T(8,128)(2,1)} %refs_0_.1, bf16[8,3584]{1,0:T(8,128)(2,1)} %refs_1_.1, bf16[8,128]{1,0:T(8,128)(2,1)} %select_reduce_fusion.refs_2_), custom_call_target="tpu_custom_call" | custom-call | tf_op jit(solution)/shard_map/pallas_call | solution.py:358
  33.6 33.8 %shard_map.103 = (bf16[256,3584]{1,0:T(8,128)(2,1)}, bf16[1,3584,1024]{2,1,0:T(8,128)(2,1)}, bf16[1,3584,1024]{2,1,0:T(8,128)(2,1)}, bf16[1,1024,3584]{2,1,0:T(8,128)(2,1)}) custom-call(f32[1,128]{1,0:T(1,128)} %compare_convert_fusion.sel_ref, bf16[256,3584]{1,0:T(8,128)(2,1)} %get-tuple-element.11.x_ref, bf16[256,3584]{1,0:T(8,128)(2,1)} %get-tuple-element.12.dy_ref, ...), custom_call_target="tpu_custom_call" | custom-call | tf_op jit(solution)/shard_map/pallas_call | solution.py:168
  67.4 0.0 copy-start
  67.4 1.5 %copy-done = bf16[256,3584]{1,0:T(8,128)(2,1)S(1)} copy-done((bf16[256,3584]{1,0:T(8,128)(2,1)S(1)}, bf16[256,3584]{1,0:T(8,128)(2,1)}, u32[]{:S(2)}) %copy-start) | copy-done | bytes 1835032
  68.9 22.2 %shard_map.104 = bf16[8,3584]{1,0:T(8,128)(2,1)S(1)} custom-call(bf16[32,8,3584]{2,1,0:T(8,128)(2,1)S(1)} %bitcast.1), custom_call_target="tpu_custom_call" | custom-call | tf_op jit(solution)/shard_map/pallas_call | solution.py:445
  91.1 0.6 copy.12
Async XLA Ops:
  67.4 1.5 %copy-start = (bf16[256,3584]{1,0:T(8,128)(2,1)S(1)}, bf16[256,3584]{1,0:T(8,128)(2,1)}, u32[]{:S(2)}) copy-start(bf16[256,3584]{1,0:T(8,128)(2,1)} %get-tuple-element.14) | copy-start | bytes 5505028

commit v3 on v2

--- a/solution.py
+++ b/solution.py
@@ -159,8 +159,8 @@
 def main_call(sel, gathered, w_gate, w_up, w_down):
     _, features, hidden = w_gate.shape
     rows = gathered[0].shape[0]
-    chunk = pick((256, 128), hidden)
-    tile = pick((512, 256, 128), features)
+    chunk = pick((512, 256, 128), hidden)
+    tile = pick((1792, 512, 256, 128), features)
     whole = lambda width: pl.BlockSpec((rows, width), lambda i: (0, 0), pipeline_mode=pl.Buffered(1))
     col = pl.BlockSpec((None, features, chunk), lambda i: (0, 0, i))
     row = pl.BlockSpec((None, chunk, features), lambda i: (0, i, 0))
@@ -375,16 +375,19 @@
     return sum(len(shape.children(order, delta)) for delta in shape.sites(order))
 
 
-def scatter_kernel(digits, axis_sizes, orders, ways, p_ref, out_ref, land, total, total32, send_sem, recv_sem):
+def scatter_kernel(digits, axis_sizes, orders, ways, p_hbm, out_ref, p_ref, land, total, total32, load_sem, send_sem, recv_sem):
     torus = Torus(digits, axis_sizes)
     parts = len(orders)
-    width = p_ref.shape[2] // parts
+    width = p_hbm.shape[2] // parts
     plan = []
     for p in range(parts):
         for number, delta in enumerate(torus.sites(orders[p])):
             plan.append((len(torus.children(orders[p], delta)), -distance(delta), p, number, delta))
     plan.sort(key=lambda entry: entry[:4])
+    load = pltpu.make_async_copy(p_hbm, p_ref, load_sem)
+    load.start()
     torus.barrier()
+    loaded = False
     later = []
     for _, _, p, number, delta in plan:
         order = orders[p]
@@ -392,7 +395,10 @@
         cols = slice(p * width, (p + 1) * width)
         root = distance(delta) == 0
         kids = torus.children(order, delta)
-        source = total if kids else p_ref
+        source = total if kids else p_hbm
+        if kids and not loaded:
+            load.wait()
+            loaded = True
         copy = None
         if not root:
             name, step = torus.parent(order, delta)
@@ -444,13 +450,15 @@
     vmem = pl.BlockSpec(memory_space=pltpu.VMEM)
     return pl.pallas_call(
         functools.partial(scatter_kernel, digits, axis_sizes, orders, ways),
-        in_specs=[vmem],
+        in_specs=[pl.BlockSpec(memory_space=pl.ANY)],
         out_specs=vmem,
         out_shape=jax.ShapeDtypeStruct((rows, features), partial.dtype),
         scratch_shapes=[
+            pltpu.VMEM((devices, rows, features), partial.dtype),
             pltpu.VMEM((len(ways), devices, rows, features), partial.dtype),
             pltpu.VMEM((devices, rows, features), partial.dtype),
             pltpu.VMEM((rows, features), jnp.float32),
+            pltpu.SemaphoreType.DMA,
             pltpu.SemaphoreType.DMA((2, count)),
             pltpu.SemaphoreType.DMA((2, len(ways), devices)),
         ],
@@ -460,9 +468,10 @@
 
 def coef_of(routes, gates):
     lanes = jnp.arange(LANES, dtype=jnp.int32)
-    hit = routes[:, :, None] == lanes[None, None, :]
-    coef = jnp.sum(jnp.where(hit, gates[:, :, None].astype(jnp.float32), 0.0), axis=1)
-    return coef.astype(jnp.bfloat16)
+    coef = jnp.zeros((routes.shape[0], LANES), gates.dtype)
+    for k in range(routes.shape[1]):
+        coef = jnp.where(routes[:, k:k + 1] == lanes, gates[:, k:k + 1], coef)
+    return coef
 
 
 def dense_per_device(digits, axis_sizes, tokens, cotangent, routes, gates, w_gate, w_up, w_down):
@@ -476,7 +485,7 @@
 def per_device(digits, axis_sizes, tokens, cotangent, routes, gates, w_gate, w_up, w_down):
     features = tokens.shape[1]
     rows = tokens.shape[0] * math.prod(axis_sizes.values())
-    chunk = pick((256, 128), w_gate.shape[2])
+    chunk = pick((512, 256, 128), w_gate.shape[2])
     need = features * (14 * rows + 24 * chunk)
     fits = need < (56 << 20) and axis_sizes["expert"] <= LANES and features % (2 * LANES) == 0
     args = (tokens, cotangent, routes, gates, w_gate, w_up, w_down)

time: 91.9 us -> 89.3 us (0.972)
  Pallas kernels: 86.4 us -> 82.5 us
  local copies, waits for them, and re-layouts: 2.12 us -> 4.67 us
  other arithmetic: 2.56 us -> 1.27 us
    pallas_call x1, Pallas kernels: 33.8 us -> 29.8 us  [main_call(): pl.pallas_call(functools.partial(main_kernel, tile), grid=(hidden // chun...]
    slice x0 -> x2, local copies, waits for them, and re-layouts: none -> 2.55 us  [coef_of(): coef = jnp.where(routes[:, k:k + 1] == lanes, gates[:, k:k + 1], coef)]
    reduce_sum x1 -> x0, other arithmetic: 1.36 us -> none  [coef_of(): jnp.sum(jnp.where(hit, gates[:, :, None].astype(jnp.float32), 0.0), axis=1)]
where the time goes in v3:
time: 89.3 us; the launch traced here: 89.1 us
  Pallas kernels  82.5 us (92%)
  local copies, waits for them, and re-layouts  4.67 us (5%)
  other arithmetic  1.27 us (1%)
    pallas_call x1, Pallas kernels, gather_call(): pl.pallas_call(functools.partial(gather_kernel, digits, axis_sizes, order...  30.4 us
    pallas_call x1, Pallas kernels, main_call(): pl.pallas_call(functools.partial(main_kernel, tile), grid=(hidden // chun...  29.8 us
    pallas_call x1, Pallas kernels, scatter_call(): pl.pallas_call(functools.partial(scatter_kernel, digits, axis_sizes, orde...  22.4 us
    slice x2, local copies, waits for them, and re-layouts, coef_of(): coef = jnp.where(routes[:, k:k + 1] == lanes, gates[:, k:k + 1], coef)  2.55 us
    unnamed x3, local copies, waits for them, and re-layouts  2.12 us

profile of v3, /device:TPU:0, one launch (start us, length us, event | category | flops | bytes accessed | tf_op | source)
XLA Modules:
  0.0 89.1 jit_solution(16673149144455285429)
XLA Ops:
  0.6 0.6 compare_convert_fusion.sel_ref
  1.2 1.3 %slice_reduce_fusion.7 = (s32[8]{0:T(128)S(1)}, s32[8]{0:T(128)S(1)}, s32[8]{0:T(128)S(1)}, s32[8]{0:T(128)S(1)}, s32[8]{0:T(128)S(1)}, /*index=5*/s32[8]{0:T(128)S(1)}, s32[8]{0:T(128)S(1)}, s32[8]{0:T(128)S(1)}) fusion(s32[8,8]{1,0:T(8,128)} %param.9), kind=kLoop, calls=%fused_computation.15 | loop fusion | bytes 512 | tf_op jit(solution)/shard_map/slice | solution.py:473
  2.5 1.3 %slice_reduce_fusion.15 = (bf16[8]{0:T(256)(128)(2,1)S(1)}, bf16[8]{0:T(256)(128)(2,1)S(1)}, bf16[8]{0:T(256)(128)(2,1)S(1)}, bf16[8]{0:T(256)(128)(2,1)S(1)}, b...) fusion(bf16[8,8]{1,0:T(8,128)(2,1)} %param.10), kind=kLoop, calls=%fused_computation.31 | loop fusion | bytes 256 | tf_op jit(solution)/shard_map/slice | solution.py:473
  3.8 0.7 fusion.refs_2_
  4.5 30.4 %shard_map.102 = (bf16[256,3584]{1,0:T(8,128)(2,1)}, bf16[256,3584]{1,0:T(8,128)(2,1)}, bf16[256,128]{1,0:T(8,128)(2,1)}) custom-call(bf16[8,3584]{1,0:T(8,128)(2,1)} %refs_0_.1, bf16[8,3584]{1,0:T(8,128)(2,1)} %refs_1_.1, bf16[8,128]{1,0:T(8,128)(2,1)} %fusion.refs_2_), custom_call_target="tpu_custom_call" | custom-call | tf_op jit(solution)/shard_map/pallas_call | solution.py:358
  34.8 29.8 %shard_map.103 = (bf16[256,3584]{1,0:T(8,128)(2,1)}, bf16[1,3584,1024]{2,1,0:T(8,128)(2,1)}, bf16[1,3584,1024]{2,1,0:T(8,128)(2,1)}, bf16[1,1024,3584]{2,1,0:T(8,128)(2,1)}) custom-call(f32[1,128]{1,0:T(1,128)} %compare_convert_fusion.sel_ref, bf16[256,3584]{1,0:T(8,128)(2,1)} %get-tuple-element.11.x_ref, bf16[256,3584]{1,0:T(8,128)(2,1)} %get-tuple-element.12.dy_ref, ...), custom_call_target="tpu_custom_call" | custom-call | tf_op jit(solution)/shard_map/pallas_call | solution.py:168
  64.6 0.0 copy-start
  64.6 1.5 %copy-done = bf16[256,3584]{1,0:T(8,128)(2,1)S(1)} copy-done((bf16[256,3584]{1,0:T(8,128)(2,1)S(1)}, bf16[256,3584]{1,0:T(8,128)(2,1)}, u32[]{:S(2)}) %copy-start) | copy-done | bytes 1835032
  66.1 22.4 %shard_map.104 = bf16[8,3584]{1,0:T(8,128)(2,1)S(1)} custom-call(bf16[32,8,3584]{2,1,0:T(8,128)(2,1)S(1)} %bitcast.1), custom_call_target="tpu_custom_call" | custom-call | tf_op jit(solution)/shard_map/pallas_call | solution.py:451
  88.4 0.6 copy.12
Async XLA Ops:
  64.6 1.5 %copy-start = (bf16[256,3584]{1,0:T(8,128)(2,1)S(1)}, bf16[256,3584]{1,0:T(8,128)(2,1)}, u32[]{:S(2)}) copy-start(bf16[256,3584]{1,0:T(8,128)(2,1)} %get-tuple-element.14) | copy-start | bytes 5505028
